TPU v7x, 32 devices: a whole 2x2x4 slice. The times are simulated.
32 devices in a mesh: group: 2 (over y), sky: 4 (over z), depth: 4 (over x, core).
Axes of the slice: x: 2, y: 2, z: 4, core: 2. Of those that a mesh axis runs over, the one named last changes fastest.
Arguments:
- convergence: float32 [512, 32, 128], P(('group', 'sky', 'depth')), parts along dimension 0, may hold values from -6 to 6
- summary_cot: float32 [512, 256], P(('group', 'sky', 'depth')), parts along dimension 0, may hold values from -6 to 6
- stem_w: bfloat16 [16, 64], replicated, may hold values from -1.5 to 1.5
- down_w: bfloat16 [256, 256], replicated, may hold values from -0.375 to 0.375
- block_w: bfloat16 [4, 2, 256, 256], replicated, may hold values from -0.375 to 0.375
- plane_ids: int32 [512, 16], P(('group', 'sky', 'depth')), parts along dimension 0, may hold values from 0 to 63, as said below
- tile_ids: int32 [512, 16], P(('group', 'sky', 'depth')), parts along dimension 0, may hold values from 0 to 31, as said below
- lens_weight: float32 [512, 16], P(('group', 'sky', 'depth')), parts along dimension 0, may hold values from 0.5 to 2
- slab_map: int32 [128], replicated, may hold values from 0 to 63, never falling along the last dimension, each value on 1 to 4 neighbouring positions
Outputs:
- density_adjoint: bfloat16 [256, 1024, 128], P(('group', 'sky'), 'depth'), parts along dimension 0
There are 2 independent parts, one for each index of `group`. A program takes and returns all parts, laid end to end along the dimension named above; an argument that names none is the same for every part. Nothing has to cross between parts.
Inputs may be any that keep to these rules, and one draw needn't show every extreme that they name: `plane_ids`: an owner is a pair (plane slab, tile range): planes l with l // 16 equal and tiles t with t // 8 equal. Of the 256 intersection entries of the 16 patches of one device (aligned blocks of 16 rows), at most 32 fall to one owner; some owner receives exactly 32 from every device's block. `tile_ids`: tile indices within a plane; see plane_ids for the bound per owner. `slab_map`: never falls along z; every plane owns at least one cell.
All inputs are finite; a program needn't handle non-finite values.
Results may differ from a plain program's by a relative error of at most 0.018.
Values may be sent and summed in bfloat16 or wider, within the bound.
A program may use at most 64 MiB of HBM per device.

v0:
```python
import jax
import jax.numpy as jnp
from jax import lax
from jax.sharding import PartitionSpec as P

PLANES = 64
TPD = 8


def summarize(maps, stem_w, down_w, block_w):
    patch_count, height, breadth = maps.shape
    chans_low = stem_w.shape[1]
    rounded = maps.astype(jnp.bfloat16)
    blocks_four = rounded.reshape(patch_count, height // 4, 4, breadth // 4, 4)
    stem_in = blocks_four.transpose(2, 4, 0, 1, 3).reshape(
        16, patch_count * (height // 4) * (breadth // 4)
    )
    stem_out = jax.nn.silu(jnp.dot(stem_w.T, stem_in, preferred_element_type=jnp.float32)).astype(
        jnp.bfloat16
    )
    coarse = stem_out.reshape(chans_low, patch_count, height // 8, 2, breadth // 8, 2)
    down_in = coarse.transpose(0, 3, 5, 1, 2, 4).reshape(
        4 * chans_low, patch_count * (height // 8) * (breadth // 8)
    )
    stream = jax.nn.silu(jnp.dot(down_w.T, down_in, preferred_element_type=jnp.float32))
    for layer in range(block_w.shape[0]):
        inner = jax.nn.silu(
            jnp.dot(
                block_w[layer, 0].T, stream.astype(jnp.bfloat16), preferred_element_type=jnp.float32
            )
        ).astype(jnp.bfloat16)
        stream = stream + jnp.dot(block_w[layer, 1].T, inner, preferred_element_type=jnp.float32)
    pooled = stream.reshape(stream.shape[0], patch_count, -1).sum(axis=2)
    return pooled.T


def body(
    convergence, summary_cot, stem_w, down_w, block_w, plane_ids, tile_ids, lens_weight, slab_map
):
    sky_count = lax.axis_size("sky")
    depth_count = lax.axis_size("depth")
    patch_here, height, breadth = convergence.shape
    pixels = height * breadth
    intersections = plane_ids.shape[1]
    slab_planes = PLANES // depth_count
    target_count = slab_planes * TPD
    _, pullback = jax.vjp(lambda values: summarize(values, stem_w, down_w, block_w), convergence)
    grads = pullback(summary_cot)[0].reshape(patch_here, pixels)
    target_rows = jnp.arange(target_count, dtype=jnp.int32)
    accelerator_list = sky_count * depth_count
    entries = patch_here * intersections
    capacity = max(2, 2 * entries // accelerator_list)
    weighted = (
        (lens_weight[:, :, None] * grads[:, None, :]).astype(jnp.bfloat16).reshape(entries, pixels)
    )
    flat_planes = plane_ids.reshape(-1)
    flat_tiles = tile_ids.reshape(-1)
    owner = flat_tiles // TPD * depth_count + flat_planes // slab_planes
    hits = (owner[:, None] == jnp.arange(accelerator_list, dtype=jnp.int32)[None, :]).astype(
        jnp.int32
    )
    before = jnp.sum((jnp.cumsum(hits, axis=0) - hits) * hits, axis=1)
    slot_index = owner * capacity + before
    local_slot = flat_planes % slab_planes * TPD + flat_tiles % TPD
    outgoing = (
        jnp.zeros((accelerator_list * capacity, pixels), jnp.bfloat16).at[slot_index].set(weighted)
    )
    outgoing = outgoing.reshape(sky_count, depth_count, capacity, pixels)
    out_slots = (
        jnp.full((accelerator_list * capacity,), -1, jnp.int32).at[slot_index].set(local_slot)
    )
    out_slots = out_slots.reshape(sky_count, depth_count, capacity)
    incoming, in_slots = (
        lax.all_to_all(
            lax.all_to_all(outgoing, "sky", split_axis=0, concat_axis=0, tiled=True),
            "depth",
            split_axis=1,
            concat_axis=1,
            tiled=True,
        ),
        lax.all_to_all(
            lax.all_to_all(out_slots, "sky", split_axis=0, concat_axis=0, tiled=True),
            "depth",
            split_axis=1,
            concat_axis=1,
            tiled=True,
        ),
    )
    selector = (in_slots.reshape(-1)[None, :] == target_rows[:, None]).astype(jnp.bfloat16)
    deposit = jnp.dot(selector, incoming.reshape(-1, pixels), preferred_element_type=jnp.float32)
    plane_block = (
        deposit.reshape(slab_planes, TPD, height, breadth)
        .transpose(0, 2, 1, 3)
        .reshape(slab_planes, height, TPD * breadth)
    )
    pencil_planes = lax.all_to_all(
        plane_block.astype(jnp.bfloat16), "depth", split_axis=2, concat_axis=0, tiled=True
    ).astype(plane_block.dtype)
    member = (slab_map[:, None] == jnp.arange(PLANES, dtype=jnp.int32)[None, :]).astype(jnp.float32)
    thickness = jnp.sum(member, axis=0)
    spread = member * (1.0 / thickness)[None, :]
    pencil = jnp.einsum("lxy,zl->xyz", pencil_planes, spread, precision=lax.Precision.HIGHEST)
    return pencil.astype(jnp.bfloat16)


def solution(mesh):
    placed = (
        P(("group", "sky", "depth"), None, None),
        P(("group", "sky", "depth"), None),
        P(),
        P(),
        P(),
        P(("group", "sky", "depth"), None),
        P(("group", "sky", "depth"), None),
        P(("group", "sky", "depth"), None),
        P(),
    )
    return jax.shard_map(
        body,
        mesh=mesh,
        in_specs=placed,
        out_specs=P(("group", "sky"), "depth", None),
        check_vma=False,
    )
```

profile of v0, /device:TPU:1, one launch (start us, length us, event | category | flops | bytes accessed | tf_op | source)
XLA Modules:
  0.0 296.8 jit_solution(13912191348763623470)
XLA Ops:
  0.0 0.8 reshape.298
  0.8 0.8 reshape.296
  1.6 0.8 reshape.299
  2.4 0.8 reshape.297
  3.1 0.8 reshape.294
  3.9 0.8 reshape.295
  4.7 0.6 reduce-window.6
  5.7 1.4 scatter_custom_fusion
  7.2 0.7 reshape.337
  7.8 5.4 %all-to-all-start = ((s32[4,1,128]{2,1,0:T(1,128)}), s32[4,1,128]{2,1,0:T(1,128)S(1)}, u32[]{:S(2)}, u32[]{:S(2)}) async-start(s32[4,1,128]{2,1,0:T(1,128)} %reshape.337), calls=%async_computation | async-start | bytes 4096 | tf_op jit(solution)/shard_map/all_to_all | solution.py:82
  13.3 1.0 convert_element_type.177
  14.7 0.7 copy.91
  16.0 2.0 multiply_convert_fusion.3
  18.5 7.2 %copy.93 = bf16[64,2,2,16,4,16]{5,4,3,2,1,0:T(4,128)(2,1)} copy(bf16[64,2,2,16,4,16]{0,2,5,1,4,3:T(2,128)(2,1)S(1)} %bitcast.196) | data formatting | bytes 1048576 | tf_op jit(solution)/shard_map/jvp()/transpose | solution.py:22
  25.7 8.3 %reshape.306 = bf16[256,1024]{1,0:T(8,128)(2,1)S(1)} reshape(bf16[64,2,2,16,4,16]{5,4,3,2,1,0:T(4,128)(2,1)} %copy.93) | data formatting | bytes 1048576 | tf_op jit(solution)/shard_map/jvp()/reshape | solution.py:22
  34.9 0.6 fusion.8
  36.8 1.2 convolution_bitcast_fusion.2
  38.1 2.7 convolution_bitcast_fusion
  40.8 1.3 copy.103
  42.1 3.4 %fusion.28 = f32[256,1024]{1,0:T(8,128)} fusion(f32[256,1024]{1,0:T(8,128)} %copy.103, f32[256,1024]{1,0:T(8,128)} %convolution_bitcast_fusion, f32[256,1024]{0,1:T(8,128)S(1)} %bitcast.199, bf16[4,2,256,256]{3,2,1,0:T(8,128)(2,1)} %param.13), kind=kOutput, calls=%fused_computation.58 | convolution fusion | flops 271843328 | bytes 4456448 | tf_op jit(solution)/shard_map/transpose(jvp())/dot_general | solution.py:28
  45.5 3.4 %fusion.23 = f32[256,1024]{1,0:T(8,128)} fusion(f32[256,1024]{1,0:T(8,128)} %fusion.28, f32[256,1024]{1,0:T(8,128)S(1)} %convolution_bitcast_fusion.2, bf16[4,2,256,256]{3,2,1,0:T(8,128)(2,1)} %param.13), kind=kOutput, calls=%fused_computation.51 | convolution fusion | flops 272105472 | bytes 4456448 | tf_op jit(solution)/shard_map/transpose(jvp())/dot_general | solution.py:28
  48.9 2.4 fusion.18
  51.3 1.2 fusion.15
  52.5 2.7 fusion.10
  55.5 7.4 %reshape.311 = f32[64,2,2,16,4,16]{5,4,3,2,1,0:T(4,128)} reshape(f32[256,1024]{1,0:T(8,128)S(1)} %copy.110) | data formatting | bytes 2097152 | tf_op jit(solution)/shard_map/transpose(jvp())/convert_element_type | solution.py:18
  63.0 8.1 %copy.111 = f32[64,16,4,2,16,2]{0,5,4,3,2,1:T(2,128)S(1)} copy(f32[64,16,4,2,16,2]{4,2,1,5,3,0:T(4,128)} %bitcast.187) | data formatting | bytes 2097152 | tf_op jit(solution)/shard_map/transpose(jvp())/convert_element_type | solution.py:18
  71.6 1.7 fusion.1
  73.7 1.0 copy.114
  75.8 6.0 %scatter_custom_fusion.1 = bf16[512,4096]{1,0:T(8,128)(2,1)} fusion(s32[256]{0:T(256)S(1)} %bitcast.205, bf16[256,4096]{1,0:T(8,128)(2,1)S(1)} %fusion.2, bf16[]{:T(256)} %constant.75.clone.1), kind=kCustom, calls=%fused_computation.7 | custom fusion | bytes 4194306 | tf_op jit(solution)/shard_map/scatter | solution.py:66
  81.8 4.9 %all-to-all-start.2 = ((bf16[4,4,32,4096]{3,2,1,0:T(8,128)(2,1)}), bf16[4,4,32,4096]{3,2,1,0:T(8,128)(2,1)}, u32[]{:S(2)}, u32[]{:S(2)}) async-start(bf16[4,4,32,4096]{3,2,1,0:T(8,128)(2,1)} %bitcast.190), calls=%async_computation.2 | async-start | bytes 8388608 | tf_op jit(solution)/shard_map/all_to_all | solution.py:75
  87.2 0.6 reduce.2
  87.8 0.7 reshape.339
  88.5 90.9 %all-to-all-done.2 = bf16[4,4,32,4096]{3,2,1,0:T(8,128)(2,1)} async-done(((bf16[4,4,32,4096]{3,2,1,0:T(8,128)(2,1)}), bf16[4,4,32,4096]{3,2,1,0:T(8,128)(2,1)}, u32[]{:S(2)}, u32[]{:S(2)}) %all-to-all-start.2) | async-done | bytes 4194336 | tf_op jit(solution)/shard_map/all_to_all | solution.py:75
  179.4 4.6 %all-to-all-start.1 = ((s32[4,1,128]{2,1,0:T(1,128)}), s32[4,1,128]{2,1,0:T(1,128)S(1)}, u32[]{:S(2)}, u32[]{:S(2)}) async-start(s32[4,1,128]{2,1,0:T(1,128)} %reshape.339), calls=%async_computation.1 | async-start | bytes 4096 | tf_op jit(solution)/shard_map/all_to_all | solution.py:81
  184.0 4.7 %copy.116 = bf16[4,4,32,4096]{3,2,0,1:T(8,128)(2,1)} copy(bf16[4,4,32,4096]{3,2,1,0:T(8,128)(2,1)} %all-to-all-done.2) | data formatting | bytes 8388608 | tf_op jit(solution)/shard_map/all_to_all | solution.py:75
  188.7 5.1 %all-to-all-start.3 = ((bf16[4,4,32,4096]{3,2,0,1:T(8,128)(2,1)}), bf16[4,4,32,4096]{3,2,0,1:T(8,128)(2,1)}, u32[]{:S(2)}, u32[]{:S(2)}) async-start(bf16[4,4,32,4096]{3,2,0,1:T(8,128)(2,1)} %copy.116), calls=%async_computation.3 | async-start | bytes 8388608 | tf_op jit(solution)/shard_map/all_to_all | solution.py:74
  193.8 0.6 reduce.3
  194.6 46.5 %all-to-all-done.3 = bf16[4,4,32,4096]{3,2,0,1:T(8,128)(2,1)} async-done(((bf16[4,4,32,4096]{3,2,0,1:T(8,128)(2,1)}), bf16[4,4,32,4096]{3,2,0,1:T(8,128)(2,1)}, u32[]{:S(2)}, u32[]{:S(2)}) %all-to-all-start.3) | async-done | bytes 4194336 | tf_op jit(solution)/shard_map/all_to_all | solution.py:74
  241.1 4.7 %copy.117 = bf16[4,4,32,4096]{3,2,1,0:T(8,128)(2,1)} copy(bf16[4,4,32,4096]{3,2,0,1:T(8,128)(2,1)} %all-to-all-done.3) | data formatting | bytes 8388608 | tf_op jit(solution)/shard_map/all_to_all | solution.py:74
  245.8 6.5 %copy.118 = bf16[4096,512]{1,0:T(8,128)(2,1)} copy(bf16[4096,512]{0,1:T(8,128)(2,1)} %bitcast.192) | data formatting | bytes 8388608 | tf_op jit(solution)/shard_map/dot_general | solution.py:90
  252.2 3.7 %fusion.5 = bf16[16,32,8,128]{3,2,1,0:T(8,128)(2,1)S(1)} fusion(bf16[32,128,512,1]{2,1,0,3:T(8,128)(2,1)} %bitcast.191, s32[16,8]{1,0:T(8,128)S(1)} %multiply_add_fusion, s32[512]{0:T(512)S(1)} %eq.69), kind=kOutput, calls=%fused_computation.17 | convolution fusion | flops 537460736 | bytes 5245440 | tf_op jit(solution)/shard_map/dot_general | solution.py:90
  255.9 3.4 %copy.137 = bf16[16,32,8,128]{1,0,3,2:T(8,128)(2,1)} copy(bf16[16,32,8,128]{3,2,1,0:T(8,128)(2,1)S(1)} %fusion.5) | data formatting | bytes 2097152 | tf_op jit(solution)/shard_map/convert_element_type | solution.py:97
  259.3 6.4 %reshape.341 = bf16[4,2,65536]{2,1,0:T(2,128)(2,1)} reshape(bf16[1024,16,32]{2,1,0:T(8,128)(2,1)} %bitcast.188) | data formatting | bytes 2097152
  265.7 4.4 %all-to-all-start.4 = ((bf16[4,2,65536]{2,1,0:T(2,128)(2,1)}), bf16[4,2,65536]{2,1,0:T(2,128)(2,1)S(1)}, u32[]{:S(2)}, u32[]{:S(2)}) async-start(bf16[4,2,65536]{2,1,0:T(2,128)(2,1)} %reshape.341), calls=%async_computation.4 | async-start | bytes 2097152 | tf_op jit(solution)/shard_map/all_to_all | solution.py:96
  270.2 13.5 %all-to-all-done.4 = bf16[4,2,65536]{2,1,0:T(2,128)(2,1)S(1)} async-done(((bf16[4,2,65536]{2,1,0:T(2,128)(2,1)}), bf16[4,2,65536]{2,1,0:T(2,128)(2,1)S(1)}, u32[]{:S(2)}, u32[]{:S(2)}) %all-to-all-start.4) | async-done | bytes 1048608 | tf_op jit(solution)/shard_map/all_to_all | solution.py:96
  283.7 3.5 %reshape.342 = bf16[1024,16,32]{2,1,0:T(8,128)(2,1)} reshape(bf16[4,2,65536]{2,1,0:T(2,128)(2,1)S(1)} %all-to-all-done.4) | data formatting | bytes 2097152
  287.2 6.1 %copy.120 = bf16[16,32,4,256]{3,0,2,1:T(8,128)(2,1)S(1)} copy(bf16[16,32,4,256]{1,0,3,2:T(8,128)(2,1)} %bitcast.189) | data formatting | bytes 2097152 | tf_op jit(solution)/shard_map/all_to_all | solution.py:96
  293.3 3.5 %convolution_convert_fusion.1 = bf16[32,256,128]{2,1,0:T(8,128)(2,1)} fusion(bf16[64,32,256]{2,0,1:T(8,128)(2,1)S(1)} %bitcast.195, f32[64]{0:T(128)S(1)} %broadcast_divide_fusion, s32[128]{0:T(128)S(1)} %copy-done.6), kind=kOutput, calls=%fused_computation.9 | convolution fusion | flops 806371328 | bytes 3146496 | tf_op jit(solution)/shard_map/lxy,zl->xyz/dot_general | solution.py:102
  (52 shorter events, 7.4 us)
Async XLA Ops:
  0.0 34.0 %copy-start = (bf16[256,256]{1,0:T(8,128)(2,1)S(1)}, bf16[256,256]{1,0:T(8,128)(2,1)}, u32[]{:S(2)}) copy-start(bf16[256,256]{1,0:T(8,128)(2,1)} %param.12) | copy-start | bytes 393220
  7.8 74.0 %all-to-all-start = ((s32[4,1,128]{2,1,0:T(1,128)}), s32[4,1,128]{2,1,0:T(1,128)S(1)}, u32[]{:S(2)}, u32[]{:S(2)}) async-start(s32[4,1,128]{2,1,0:T(1,128)} %reshape.337), calls=%async_computation | async-start | bytes 4096 | tf_op jit(solution)/shard_map/all_to_all | solution.py:82
  25.7 8.6 %copy-start.3 = (bf16[4,2,256,256]{3,2,1,0:T(8,128)(2,1)S(1)}, bf16[4,2,256,256]{3,2,1,0:T(8,128)(2,1)}, u32[]{:S(2)}) copy-start(bf16[4,2,256,256]{3,2,1,0:T(8,128)(2,1)} %param.13) | copy-start | bytes 3145732
  34.4 1.2 copy-start.2
  34.9 1.0 copy-start.8
  36.8 3.9 %copy-start.4 = (f32[16,256]{1,0:T(8,128)S(1)}, f32[16,256]{1,0:T(8,128)}, u32[]{:S(2)}) copy-start(f32[16,256]{1,0:T(8,128)} %param.10) | copy-start | bytes 49156
  63.0 8.7 %copy-start.7 = (bf16[16,64]{1,0:T(8,128)(2,1)S(1)}, bf16[16,64]{1,0:T(8,128)(2,1)}, u32[]{:S(2)}) copy-start(bf16[16,64]{1,0:T(8,128)(2,1)} %param.11) | copy-start | bytes 6148
  73.4 1.9 copy-start.5
  81.8 97.6 %all-to-all-start.2 = ((bf16[4,4,32,4096]{3,2,1,0:T(8,128)(2,1)}), bf16[4,4,32,4096]{3,2,1,0:T(8,128)(2,1)}, u32[]{:S(2)}, u32[]{:S(2)}) async-start(bf16[4,4,32,4096]{3,2,1,0:T(8,128)(2,1)} %bitcast.190), calls=%async_computation.2 | async-start | bytes 8388608 | tf_op jit(solution)/shard_map/all_to_all | solution.py:75
  179.4 9.3 %all-to-all-start.1 = ((s32[4,1,128]{2,1,0:T(1,128)}), s32[4,1,128]{2,1,0:T(1,128)S(1)}, u32[]{:S(2)}, u32[]{:S(2)}) async-start(s32[4,1,128]{2,1,0:T(1,128)} %reshape.339), calls=%async_computation.1 | async-start | bytes 4096 | tf_op jit(solution)/shard_map/all_to_all | solution.py:81
  188.7 52.4 %all-to-all-start.3 = ((bf16[4,4,32,4096]{3,2,0,1:T(8,128)(2,1)}), bf16[4,4,32,4096]{3,2,0,1:T(8,128)(2,1)}, u32[]{:S(2)}, u32[]{:S(2)}) async-start(bf16[4,4,32,4096]{3,2,0,1:T(8,128)(2,1)} %copy.116), calls=%async_computation.3 | async-start | bytes 8388608 | tf_op jit(solution)/shard_map/all_to_all | solution.py:74
  259.3 10.8 %copy-start.6 = (s32[128]{0:T(128)S(1)}, s32[128]{0:T(128)}, u32[]{:S(2)}) copy-start(s32[128]{0:T(128)} %param.17) | copy-start | bytes 1540
  265.7 18.0 %all-to-all-start.4 = ((bf16[4,2,65536]{2,1,0:T(2,128)(2,1)}), bf16[4,2,65536]{2,1,0:T(2,128)(2,1)S(1)}, u32[]{:S(2)}, u32[]{:S(2)}) async-start(bf16[4,2,65536]{2,1,0:T(2,128)(2,1)} %reshape.341), calls=%async_computation.4 | async-start | bytes 2097152 | tf_op jit(solution)/shard_map/all_to_all | solution.py:96
  287.2 9.6 %copy-start.1 = (bf16[256,256]{1,0:T(8,128)(2,1)S(1)}, bf16[256,256]{1,0:T(8,128)(2,1)}, u32[]{:S(2)}) copy-start(bf16[256,256]{1,0:T(8,128)(2,1)} %param.12) | copy-start | bytes 393220
where the time goes:
time: 299 us; the launch traced here: 297 us
  waiting for transfers between devices  151 us (51%)
  local copies, waits for them, and re-layouts  87.5 us (29%)
  matrix products  30.2 us (10%)
  starting transfers between devices  24.4 us (8%)
  other arithmetic  3.42 us (1%)
    all_to_all x1, waiting for transfers between devices, body(): lax.all_to_all(outgoing, 'sky', split_axis=0, concat_axis=0, tiled=True)  90.9 us
    all_to_all x1, waiting for transfers between devices, body(): lax.all_to_all(lax.all_to_all(outgoing, 'sky', split_axis=0, concat_axis=...  46.5 us
    convert_element_type x5, local copies, waits for them, and re-layouts, summarize(): jax.nn.silu(jnp.dot(stem_w.T, stem_in, preferred_element_type=jnp.float32))  16.9 us
    dot_general x7, matrix products, summarize(): jnp.dot(block_w[layer, 0].T, stream.astype(jnp.bfloat16), preferred_eleme...  13.9 us
    all_to_all x1, waiting for transfers between devices, body(): lax.all_to_all(plane_block.astype(jnp.bfloat16), 'depth', split_axis=2, c...  13.5 us
    unnamed x24, local copies, waits for them, and re-layouts  11.9 us
    reshape x1, local copies, waits for them, and re-layouts, summarize(): coarse.transpose(0, 3, 5, 1, 2, 4)  8.27 us
    transpose x1, local copies, waits for them, and re-layouts, summarize(): coarse.transpose(0, 3, 5, 1, 2, 4)  7.22 us
  transfers between devices with their start and end apart: 5, of which 3 were waited for; matrix products, arithmetic and copies ran while one was open for 25% of the time, Pallas kernels for 0%

commit v1 on v0

--- a/solution.py
+++ b/solution.py
@@ -34,7 +34,7 @@
     return pooled.T
 
 
-def body(
+def body_exchange(
     convergence, summary_cot, stem_w, down_w, block_w, plane_ids, tile_ids, lens_weight, slab_map
 ):
     sky_count = lax.axis_size("sky")
@@ -103,6 +103,52 @@
     return pencil.astype(jnp.bfloat16)
 
 
+def gradients(convergence, summary_cot, stem_w, down_w, block_w):
+    _, pullback = jax.vjp(lambda values: summarize(values, stem_w, down_w, block_w), convergence)
+    return pullback(summary_cot)[0]
+
+
+def body_gather(
+    convergence, summary_cot, stem_w, down_w, block_w, plane_ids, tile_ids, lens_weight, slab_map
+):
+    depth_count = lax.axis_size("depth")
+    tiles_here = TPD // depth_count
+    first_tile = lax.axis_index("sky") * TPD + lax.axis_index("depth") * tiles_here
+    patch_here, height, breadth = convergence.shape
+    tile_count = lax.axis_size("sky") * TPD
+    code = (plane_ids * tile_count + tile_ids).astype(jnp.float32)
+    table = lax.all_gather(
+        jnp.concatenate([code, lens_weight], axis=1), ("sky", "depth"), axis=0, tiled=True
+    )
+    ov = plane_ids.shape[1]
+    codes, weights = table[:, :ov].astype(jnp.int32), table[:, ov:]
+    thickness = jnp.sum((slab_map[:, None] == slab_map[None, :]).astype(jnp.float32), axis=0)
+    wanted = (
+        slab_map[None, :] * tile_count
+        + first_tile
+        + jnp.arange(tiles_here, dtype=jnp.int32)[:, None]
+    )
+    mixing = jnp.sum(
+        jnp.where(codes[:, :, None, None] == wanted[None, None], weights[:, :, None, None], 0.0),
+        axis=1,
+    )
+    mixing = (mixing * (1.0 / thickness)[None, None, :]).astype(jnp.bfloat16)
+    grads = gradients(convergence, summary_cot, stem_w, down_w, block_w)
+    everyone = lax.all_gather(
+        grads.astype(jnp.bfloat16), ("sky", "depth"), axis=0, tiled=True
+    )
+    pencil = jnp.einsum("pxy,ptz->xtyz", everyone, mixing, preferred_element_type=jnp.float32)
+    return pencil.astype(jnp.bfloat16).reshape(height, tiles_here * breadth, -1)
+
+
+def body(convergence, summary_cot, stem_w, down_w, block_w, plane_ids, *rest):
+    group = lax.axis_size("sky") * lax.axis_size("depth")
+    gathered = group * convergence.shape[0]
+    exchanged = 2 * plane_ids.size
+    form = body_gather if gathered <= exchanged else body_exchange
+    return form(convergence, summary_cot, stem_w, down_w, block_w, plane_ids, *rest)
+
+
 def solution(mesh):
     placed = (
         P(("group", "sky", "depth"), None, None),

time: 299 us -> 124 us (0.41)
  waiting for transfers between devices: 151 us -> 18.3 us
  local copies, waits for them, and re-layouts: 87.5 us -> 39.1 us
  starting transfers between devices: 24.4 us -> 0.01 us
  blocking collectives: 0 us -> 23.6 us
  between operations: 0.29 us -> 13.7 us
  matrix products: 30.2 us -> 25.7 us
    all_to_all x5 -> x0, waiting for transfers between devices: 151 us -> none  [the longest x1 90.9 us: body(): lax.all_to_all(outgoing, 'sky', split_axis=0, concat_axis=0, tiled=True)]
    all_to_all x5 -> x0, starting transfers between devices: 24.4 us -> none  [the longest x1 5.42 us: body(): lax.all_to_all(out_slots, 'sky', split_axis=0, concat_axis=0, tiled=True)]
    all_gather x0 -> x1, blocking collectives: none -> 23.6 us  [body_gather(): lax.all_gather(jnp.concatenate([code, lens_weight], axis=1), ('sky', 'dep...]
    all_gather x0 -> x1, waiting for transfers between devices: none -> 18.2 us  [body_gather(): lax.all_gather(grads.astype(jnp.bfloat16), ('sky', 'depth'), axis=0, tile...]
    all_to_all x6 -> x0, local copies, waits for them, and re-layouts: 15.9 us -> none  [the longest x1 6.09 us: body(): lax.all_to_all(plane_block.astype(jnp.bfloat16), 'depth', split_axis=2, c...]
    unnamed x24 -> x22, local copies, waits for them, and re-layouts: 11.9 us -> 1.42 us
    scatter x2 -> x0, local copies, waits for them, and re-layouts: 7.43 us -> none  [the longest x1 6.04 us: body(): jnp.zeros((accelerator_list * capacity, pixels), jnp.bfloat16)]
    dot_general x1 -> x0, local copies, waits for them, and re-layouts: 6.46 us -> none  [body(): jnp.dot(selector, incoming.reshape(-1, pixels), preferred_element_type=jn...]
  transfers between devices with their start and end apart: 5 -> 1, of which waited for: 3 -> 1; matrix products, arithmetic and copies ran while one was open for 25% -> 2% of each run, Pallas kernels for 0% -> 0%
where the time goes in v1:
time: 124 us; the launch traced here: 123 us
  local copies, waits for them, and re-layouts  39.1 us (32%)
  matrix products  25.7 us (21%)
  blocking collectives  23.6 us (19%)
  waiting for transfers between devices  18.3 us (15%)
  between operations  13.7 us (11%)
  other arithmetic  3 us (2%)
    all_gather x1, blocking collectives, body_gather(): lax.all_gather(jnp.concatenate([code, lens_weight], axis=1), ('sky', 'dep...  23.6 us
    all_gather x1, waiting for transfers between devices, body_gather(): lax.all_gather(grads.astype(jnp.bfloat16), ('sky', 'depth'), axis=0, tile...  18.2 us
    convert_element_type x5, local copies, waits for them, and re-layouts, summarize(): jax.nn.silu(jnp.dot(stem_w.T, stem_in, preferred_element_type=jnp.float32))  16.7 us
    dot_general x7, matrix products, summarize(): jnp.dot(block_w[layer, 0].T, stream.astype(jnp.bfloat16), preferred_eleme...  14 us
    reshape x1, local copies, waits for them, and re-layouts, summarize(): coarse.transpose(0, 3, 5, 1, 2, 4)  8.18 us
    transpose x1, local copies, waits for them, and re-layouts, summarize(): coarse.transpose(0, 3, 5, 1, 2, 4)  7.1 us
    dot_general x2, matrix products, summarize(): jnp.dot(stem_w.T, stem_in, preferred_element_type=jnp.float32)  3.8 us
    dot_general x2, matrix products, summarize(): jnp.dot(down_w.T, down_in, preferred_element_type=jnp.float32)  3.06 us
  transfers between devices with their start and end apart: 1, of which 1 were waited for; matrix products, arithmetic and copies ran while one was open for 2% of the time, Pallas kernels for 0%

profile of v1, /device:TPU:1, one launch (start us, length us, event | category | flops | bytes accessed | tf_op | source)
XLA Modules:
  0.0 123.4 jit_solution(3986235348763243319)
XLA Ops:
  6.5 1.0 convert_element_type.154
  7.5 0.5 copy.82
  8.1 0.7 copy.83
  8.8 0.5 reshape.62
  9.3 2.0 %multiply_convert_fusion.3 = (bf16[64,4096]{1,0:T(8,128)(2,1)S(1)}, f32[64,4096]{1,0:T(8,128)}) fusion(bf16[16,64]{1,0:T(8,128)(2,1)} %param.11, bf16[16,4096]{1,0:T(8,128)(2,1)S(1)} %reshape.62), kind=kOutput, calls=%fused_computation.89 | convolution fusion | flops 9699328 | bytes 1705984 | tf_op jit(solution)/shard_map/jvp()/dot_general | solution.py:18
  11.3 0.5 copy.84
  11.8 0.0 copy-start.4
  11.8 7.1 %copy.85 = bf16[64,2,2,16,4,16]{5,4,3,2,1,0:T(4,128)(2,1)} copy(bf16[64,2,2,16,4,16]{0,2,5,1,4,3:T(2,128)(2,1)S(1)} %bitcast.147) | data formatting | bytes 1048576 | tf_op jit(solution)/shard_map/jvp()/transpose | solution.py:22
  18.9 8.2 %reshape.64 = bf16[256,1024]{1,0:T(8,128)(2,1)S(1)} reshape(bf16[64,2,2,16,4,16]{5,4,3,2,1,0:T(4,128)(2,1)} %copy.85) | data formatting | bytes 1048576 | tf_op jit(solution)/shard_map/jvp()/reshape | solution.py:22
  27.1 0.1 broadcast_in_dim.16
  27.2 0.3 copy.95
  27.6 0.0 copy-start.3
  27.6 0.3 convolution_bitcast_fusion.7
  27.9 0.0 copy-start.2
  27.9 1.6 %convolution_bitcast_fusion.6 = f32[256,1024]{1,0:T(8,128)S(1)} fusion(f32[256,1024]{1,0:T(8,128)S(1)} %convolution_bitcast_fusion.7, bf16[4,2,256,256]{3,2,1,0:T(8,128)(2,1)} %param.13), kind=kOutput, calls=%fused_computation.21 | convolution fusion | flops 135528448 | bytes 2228224 | tf_op jit(solution)/shard_map/jvp()/dot_general | solution.py:28
  29.5 0.6 fusion.7
  30.1 0.4 copy-done.10
  30.5 0.3 convolution_bitcast_fusion.4
  30.9 0.5 fusion.6
  31.4 1.0 copy-done.1
  32.4 1.3 %convolution_bitcast_fusion.2 = f32[256,1024]{1,0:T(8,128)} fusion(f32[256,1024]{1,0:T(8,128)S(1)} %fusion.6, bf16[4,2,256,256]{3,2,1,0:T(8,128)(2,1)S(1)} %copy-done.3), kind=kOutput, calls=%fused_computation.15 | convolution fusion | flops 134479872 | bytes 2228224 | tf_op jit(solution)/shard_map/jvp()/dot_general | solution.py:28
  33.7 3.3 %convolution_bitcast_fusion = f32[256,1024]{1,0:T(8,128)} fusion(f32[256,1024]{1,0:T(8,128)} %copy-done.1, f32[256,1024]{1,0:T(8,128)} %convolution_bitcast_fusion.2, bf16[4,2,256,256]{3,2,1,0:T(8,128)(2,1)} %param.13), kind=kOutput, calls=%fused_computation.12 | convolution fusion | flops 270270464 | bytes 3407872 | tf_op jit(solution)/shard_map/jvp()/dot_general | solution.py:28
  37.0 3.0 %fusion.27 = f32[256,1024]{1,0:T(8,128)} fusion(f32[256,1024]{1,0:T(8,128)S(1)} %copy.95, f32[256,1024]{1,0:T(8,128)} %convolution_bitcast_fusion, f32[256,1024]{0,1:T(8,128)S(1)} %bitcast.151, bf16[4,2,256,256]{3,2,1,0:T(8,128)(2,1)} %param.13), kind=kOutput, calls=%fused_computation.52 | convolution fusion | flops 271843328 | bytes 4456448 | tf_op jit(solution)/shard_map/transpose(jvp())/dot_general | solution.py:28
  40.0 2.7 %fusion.22 = f32[256,1024]{1,0:T(8,128)S(1)} fusion(f32[256,1024]{1,0:T(8,128)} %fusion.27, f32[256,1024]{1,0:T(8,128)} %convolution_bitcast_fusion.2, bf16[4,2,256,256]{3,2,1,0:T(8,128)(2,1)} %param.13), kind=kOutput, calls=%fused_computation.45 | convolution fusion | flops 272105472 | bytes 4456448 | tf_op jit(solution)/shard_map/transpose(jvp())/dot_general | solution.py:28
  42.8 1.7 %fusion.17 = f32[256,1024]{1,0:T(8,128)S(1)} fusion(f32[256,1024]{1,0:T(8,128)S(1)} %fusion.22, f32[256,1024]{1,0:T(8,128)S(1)} %convolution_bitcast_fusion.4, bf16[4,2,256,256]{3,2,1,0:T(8,128)(2,1)} %param.13), kind=kOutput, calls=%fused_computation.38 | convolution fusion | flops 272105472 | bytes 4456448 | tf_op jit(solution)/shard_map/transpose(jvp())/dot_general | solution.py:28
  44.4 1.2 fusion.14
  45.7 2.7 %fusion.9 = f32[256,1024]{0,1:T(8,128)S(1)} fusion(bf16[256,256]{1,0:T(8,128)(2,1)S(1)} %copy-done, f32[256,1024]{1,0:T(8,128)} %copy-done.2, f32[256,1024]{1,0:T(8,128)S(1)} %fusion.17, f32[256,1024]{1,0:T(8,128)} %copy-done.10, f32[256,1024]{1,0:T(8,128)S(1)} %fusion.14, bf16[4,2,256,256]{3,2,1,0:T(8,128)(2,1)} %param.13), kind=kOutput, calls=%fused_computation.27 | convolution fusion | flops 274464768 | bytes 5505024 | tf_op jit(solution)/shard_map/transpose(jvp())/dot_general | solution.py:25
  48.4 0.3 copy.102
  48.7 7.2 %reshape.69 = f32[64,2,2,16,4,16]{5,4,3,2,1,0:T(4,128)} reshape(f32[256,1024]{1,0:T(8,128)S(1)} %copy.102) | data formatting | bytes 2097152 | tf_op jit(solution)/shard_map/transpose(jvp())/convert_element_type | solution.py:18
  56.0 8.1 %copy.103 = f32[64,16,4,2,16,2]{0,5,4,3,2,1:T(2,128)S(1)} copy(f32[64,16,4,2,16,2]{4,2,1,5,3,0:T(4,128)} %bitcast.145) | data formatting | bytes 2097152 | tf_op jit(solution)/shard_map/transpose(jvp())/convert_element_type | solution.py:18
  64.0 0.6 copy.104
  64.6 0.0 copy-start.5
  64.6 0.0 copy-start.6
  64.7 0.0 copy-start.7
  64.7 0.0 copy-start.9
  64.7 1.8 %fusion = bf16[16,4096]{1,0:T(8,128)(2,1)S(1)} fusion(bf16[16,64]{1,0:T(8,128)(2,1)S(1)} %copy-done.8, f32[64,4096]{1,0:T(8,128)} %get-tuple-element.8, f32[64,4096]{1,0:T(8,128)S(1)} %copy.104), kind=kOutput, calls=%fused_computation.1 | convolution fusion | flops 10813440 | bytes 2230272 | tf_op jit(solution)/shard_map/transpose(jvp())/dot_general | solution.py:18
  66.4 0.4 reshape.65
  66.8 0.8 copy.106
  67.6 1.0 copy.107
  68.6 0.0 all-gather.2.cloned.1.call-update
  68.7 0.1 pad_maximum_fusion
  68.8 23.6 %all_gather.6 = f32[256,32]{1,0:T(8,128)S(1)} all-gather(f32[16,32]{1,0:T(8,128)S(1)} %pad_maximum_fusion), channel_id=1, replica_groups=mesh['group'=2,'sky'=4,'depth'=4] {'sky','depth'}, dimensions={0}, use_global_device_ids=true | all-gather | bytes 34816 | tf_op jit(solution)/shard_map/all_gather | solution.py:120
  92.4 0.1 convert_reduce_fusion
  92.5 0.1 slice_convert_fusion
  92.6 1.7 %select_reduce_fusion = f32[256,2,128]{2,1,0:T(2,128)S(1)} fusion(f32[256,16]{1,0:T(8,128)S(1)} %get-tuple-element.6, s32[2,128]{1,0:T(2,128)S(1)} %iota_add_fusion, s32[256,16]{1,0:T(8,128)S(1)} %get-tuple-element.5), kind=kLoop, calls=%fused_computation.2 | loop fusion | flops 3080192 | bytes 295936 | tf_op jit(solution)/shard_map/reduce_sum | solution.py:131
  94.3 18.2 %all-gather.2.cloned.1.call-done = bf16[256,32,128]{2,0,1:T(8,128)(2,1)} async-done(((bf16[16,32,128]{2,0,1:T(8,128)(2,1)}), bf16[256,32,128]{2,0,1:T(8,128)(2,1)}) %all-gather.2.cloned.1.call-update) | async-done | bytes 2097168 | tf_op jit(solution)/shard_map/all_gather | solution.py:137
  112.6 2.5 %convert_bitcast_fusion = bf16[32,2,128,128]{3,2,0,1:T(8,128)(2,1)S(1)} fusion(bf16[256,32,128]{2,0,1:T(8,128)(2,1)} %all-gather.2.cloned.1.call-done, f32[256,2,128]{2,1,0:T(2,128)S(1)} %select_reduce_fusion, f32[128]{0:T(128)S(1)} %broadcast_divide_fusion), kind=kOutput, calls=%fused_computation.5 | convolution fusion | flops 538050560 | bytes 4456960 | tf_op jit(solution)/shard_map/pxy,ptz->xtyz/dot_general | solution.py:140
  115.1 1.5 %copy.108 = bf16[32,2,128,128]{3,2,1,0:T(8,128)(2,1)} copy(bf16[32,2,128,128]{3,2,0,1:T(8,128)(2,1)S(1)} %convert_bitcast_fusion) | data formatting | bytes 4194304 | tf_op jit(solution)/shard_map/convert_element_type | solution.py:141
  (18 shorter events, 0.0 us)
Async XLA Ops:
  6.5 21.0 %copy-start = (bf16[256,256]{1,0:T(8,128)(2,1)S(1)}, bf16[256,256]{1,0:T(8,128)(2,1)}, u32[]{:S(2)}) copy-start(bf16[256,256]{1,0:T(8,128)(2,1)} %param.12) | copy-start | bytes 393220
  6.5 106.0 %all-gather.2.cloned.1.call-start = ((), (), s32[]{:S(2)}) async-start(), calls=%async_computation | async-start | bytes 2228224 | tf_op jit(solution)/shard_map/all_gather | solution.py:137
  11.8 15.3 %copy-start.4 = (f32[16,256]{1,0:T(8,128)S(1)}, f32[16,256]{1,0:T(8,128)}, u32[]{:S(2)}) copy-start(f32[16,256]{1,0:T(8,128)} %param.10) | copy-start | bytes 49156
  27.6 1.9 %copy-start.3 = (bf16[4,2,256,256]{3,2,1,0:T(8,128)(2,1)S(1)}, bf16[4,2,256,256]{3,2,1,0:T(8,128)(2,1)}, u32[]{:S(2)}) copy-start(bf16[4,2,256,256]{3,2,1,0:T(8,128)(2,1)} %param.13) | copy-start | bytes 3145732
  27.9 2.2 %copy-start.2 = (f32[256,1024]{1,0:T(8,128)}, f32[256,1024]{1,0:T(8,128)S(1)}, u32[]{:S(2)}) copy-start(f32[256,1024]{1,0:T(8,128)S(1)} %convolution_bitcast_fusion.7) | copy-start | bytes 3145732
  29.5 1.0 copy-start.10
  31.4 1.0 copy-start.1
  56.0 8.7 %copy-start.8 = (bf16[16,64]{1,0:T(8,128)(2,1)S(1)}, bf16[16,64]{1,0:T(8,128)(2,1)}, u32[]{:S(2)}) copy-start(bf16[16,64]{1,0:T(8,128)(2,1)} %param.11) | copy-start | bytes 6148
  64.6 4.0 %copy-start.5 = (s32[16,16]{1,0:T(8,128)S(1)}, s32[16,16]{1,0:T(8,128)}, u32[]{:S(2)}) copy-start(s32[16,16]{1,0:T(8,128)} %param.15) | copy-start | bytes 3076
  64.6 4.0 %copy-start.6 = (s32[16,16]{1,0:T(8,128)S(1)}, s32[16,16]{1,0:T(8,128)}, u32[]{:S(2)}) copy-start(s32[16,16]{1,0:T(8,128)} %param.14) | copy-start | bytes 3076
  64.7 4.0 %copy-start.7 = (f32[16,16]{1,0:T(8,128)S(1)}, f32[16,16]{1,0:T(8,128)}, u32[]{:S(2)}) copy-start(f32[16,16]{1,0:T(8,128)} %param.16) | copy-start | bytes 3076
  64.7 27.7 %copy-start.9 = (s32[128]{0:T(128)S(1)}, s32[128]{0:T(128)}, u32[]{:S(2)}) copy-start(s32[128]{0:T(128)} %param.17) | copy-start | bytes 1540
Sparse Core Ops, SparseCore 0:
  68.7 43.7 all-gather.1

commit v2 on v0

--- a/solution.py
+++ b/solution.py
@@ -1,6 +1,10 @@
+import functools
+
 import jax
 import jax.numpy as jnp
 from jax import lax
+from jax.experimental import pallas as pl
+from jax.experimental.pallas import tpu as pltpu
 from jax.sharding import PartitionSpec as P
 
 PLANES = 64
@@ -34,7 +38,7 @@
     return pooled.T
 
 
-def body(
+def body_exchange(
     convergence, summary_cot, stem_w, down_w, block_w, plane_ids, tile_ids, lens_weight, slab_map
 ):
     sky_count = lax.axis_size("sky")
@@ -103,6 +107,335 @@
     return pencil.astype(jnp.bfloat16)
 
 
+MESH = pl.DeviceIdType.MESH
+
+
+def sigmoid(v):
+    return 0.5 * jnp.tanh(0.5 * v) + 0.5
+
+
+def silu_pair(v):
+    gate = sigmoid(v)
+    value = v * gate
+    return value, gate + value * (1.0 - gate)
+
+
+def dot(a, b):
+    return jnp.dot(a, b, preferred_element_type=jnp.float32)
+
+
+def dot_t(a, b):
+    return lax.dot_general(a, b, (((1,), (1,)), ((), ())), preferred_element_type=jnp.float32)
+
+
+def pencil_kernel(
+    sizes,
+    conv,
+    cot,
+    stem_w,
+    down_w,
+    block_w,
+    planes,
+    tiles,
+    lens,
+    slab,
+    out,
+    grads,
+    table,
+    taps,
+    mixing,
+    send_sem,
+    recv_sem,
+    table_send,
+    table_recv,
+):
+    sky_count, depth_count, tile_count = sizes
+    bf = jnp.bfloat16
+    patch, height, width = conv.shape
+    low, wide = stem_w.shape[1], down_w.shape[0]
+    chunks, across = height // 8, width // 8
+    ov = planes.shape[1]
+    tiles_here = TPD // depth_count
+    group = sky_count * depth_count
+    sky, depth = lax.axis_index("sky"), lax.axis_index("depth")
+    core = lax.rem(depth, 2)
+    partner = depth + 1 - 2 * core
+    columns = depth_count // 2
+    me = sky * depth_count + depth
+
+    def shifted(by_sky, by_depth):
+        return lax.rem(sky + by_sky, sky_count), lax.rem(depth + by_depth, depth_count)
+
+    barrier = pltpu.get_barrier_semaphore()
+    for step in range(1, group):
+        to_sky, to_depth = shifted(step // depth_count, step % depth_count)
+        pl.semaphore_signal(
+            barrier, inc=1, device_id={"sky": to_sky, "depth": to_depth}, device_id_type=MESH
+        )
+
+    table[me, :, 0:ov] = (planes[...] * tile_count + tiles[...]).astype(jnp.float32)
+    table[me, :, ov : 2 * ov] = lens[...]
+
+    row = lax.broadcasted_iota(jnp.int32, (8 * width, patch), 0)
+    tap = ((row >> (width.bit_length() - 1)) & 3) * 4 + (row & 3)
+    pick = (tap == lax.broadcasted_iota(jnp.int32, (8 * width, patch), 1)).astype(bf)
+    widen = (
+        lax.broadcasted_iota(jnp.int32, (low, wide), 1) >> 2
+        == lax.broadcasted_iota(jnp.int32, (low, wide), 0)
+    ).astype(bf)
+    spread = dot(pick, dot(stem_w[...], widen).astype(bf))
+    row = lax.broadcasted_iota(jnp.int32, (8 * width, wide), 0)
+    lane = lax.broadcasted_iota(jnp.int32, (8 * width, wide), 1)
+    row_half = row >> (width.bit_length() + 1)
+    same = (row_half == ((lane >> 1) & 1)) & (((row >> 2) & 1) == (lane & 1))
+    taps[...] = jnp.where(same, spread, 0.0).astype(bf)
+
+    pl.semaphore_wait(barrier, group - 1)
+
+    def table_copy(step):
+        to_sky, to_depth = shifted(step // depth_count, step % depth_count)
+        return pltpu.make_async_remote_copy(
+            src_ref=table.at[me],
+            dst_ref=table.at[me],
+            send_sem=table_send.at[step],
+            recv_sem=table_recv.at[me],
+            device_id={"sky": to_sky, "depth": to_depth},
+            device_id_type=MESH,
+        )
+
+    for step in range(1, group):
+        table_copy(step).start()
+
+    positions = across * patch
+    lane_group = lax.broadcasted_iota(jnp.int32, (patch, width), 1) >> 3
+
+    def compute(q):
+        streams = []
+        for r in range(8):
+            rows = conv[:, pl.ds(q * 8 + r, 1), :].reshape(patch, width)
+            streams.append(
+                jnp.concatenate(
+                    [jnp.where(lane_group == b, rows, 0.0).astype(bf) for b in range(across)],
+                    axis=0,
+                )
+            )
+        stem_in = jnp.concatenate(streams, axis=1)
+        stem, stem_slope = silu_pair(dot(stem_in, taps[...]))
+        stream, down_slope = silu_pair(dot(stem.astype(bf), down_w[...]))
+        slopes = []
+        for layer in range(block_w.shape[0]):
+            inner, slope = silu_pair(dot(stream.astype(bf), block_w[layer, 0]))
+            slopes.append(slope)
+            if layer + 1 < block_w.shape[0]:
+                stream = stream + dot(inner.astype(bf), block_w[layer, 1])
+        flow = jnp.concatenate([cot[...]] * across, axis=0)
+        for layer in reversed(range(block_w.shape[0])):
+            inner = dot_t(flow.astype(bf), block_w[layer, 1]).astype(bf).astype(jnp.float32)
+            inner = (inner * slopes[layer]).astype(bf)
+            flow = flow + dot_t(inner, block_w[layer, 0]).astype(bf).astype(jnp.float32)
+        flow = dot_t((flow * down_slope).astype(bf), down_w[...]).astype(bf).astype(jnp.float32)
+        flow = (flow * stem_slope).astype(bf)
+        for r in range(8):
+            back = dot_t(flow, taps[pl.ds(r * width, width), :])
+            total = jnp.zeros((patch, width), jnp.float32)
+            for b in range(across):
+                total = jnp.where(lane_group == b, back[b * patch : (b + 1) * patch], total)
+            grads[me, q * 8 + r] = total.astype(bf)
+
+    def block_copy(q, source, to_sky, to_depth, slot):
+        block = grads.at[source, pl.ds(q * 8, 8)]
+        return pltpu.make_async_remote_copy(
+            src_ref=block,
+            dst_ref=block,
+            send_sem=send_sem.at[slot, q],
+            recv_sem=recv_sem.at[source, q],
+            device_id={"sky": to_sky, "depth": to_depth},
+            device_id_type=MESH,
+        )
+
+    def index(a, b):
+        return a * depth_count + b
+
+    def plan():
+        own, relay, last = [], [], []
+        slot = 0
+        for step in range(1, sky_count):
+            own.append((me, lax.rem(sky + step, sky_count), depth, slot))
+            slot += 1
+        for step in range(1, columns):
+            own.append((me, sky, lax.rem(depth + 2 * step, depth_count), slot))
+            slot += 1
+        own.append((me, sky, partner, slot))
+        slot += 1
+        for step in range(1, sky_count):
+            source = index(lax.rem(sky + step, sky_count), depth)
+            sends = []
+            for other in range(1, columns):
+                sends.append((source, sky, lax.rem(depth + 2 * other, depth_count), slot))
+                slot += 1
+            sends.append((source, sky, partner, slot))
+            slot += 1
+            relay.append((source, sends))
+        for step in range(sky_count):
+            for other in range(1, columns):
+                source = index(
+                    lax.rem(sky + step, sky_count), lax.rem(depth + 2 * other, depth_count)
+                )
+                last.append((source, [(source, sky, partner, slot)]))
+                slot += 1
+        final = [
+            index(lax.rem(sky + step, sky_count), lax.rem(partner + 2 * other, depth_count))
+            for step in range(sky_count)
+            for other in range(columns)
+        ]
+        return own, relay, last, final
+
+    own, relay, last, final = plan()
+
+    def arrived(q, source):
+        block_copy(q, source, sky, partner, 0).wait_recv()
+
+    def forward(q, items):
+        for source, sends in items:
+            arrived(q, source)
+            for send in sends:
+                block_copy(q, *send).start()
+
+    def mix_tables():
+        for step in range(1, group):
+            a, b = shifted(step // depth_count, step % depth_count)
+            pltpu.make_async_remote_copy(
+                src_ref=table.at[me],
+                dst_ref=table.at[index(a, b)],
+                send_sem=table_send.at[step],
+                recv_sem=table_recv.at[index(a, b)],
+                device_id={"sky": a, "depth": b},
+                device_id_type=MESH,
+            ).wait_recv()
+        first_tile = (sky * TPD + depth * tiles_here).astype(jnp.float32)
+        cells = slab[...].astype(jnp.float32)
+        cell_count = cells.shape[1]
+        square = jnp.broadcast_to(cells, (cell_count, cell_count))
+        thickness = jnp.sum((square == square.T).astype(jnp.float32), axis=0, keepdims=True)
+        wanted = jnp.concatenate(
+            [cells * float(tile_count) + first_tile + float(t) for t in range(tiles_here)], axis=1
+        )
+        inverse = jnp.concatenate([1.0 / thickness] * tiles_here, axis=1)
+
+        @pl.loop(0, group)
+        def _(device):
+            entries = table[device]
+            total = jnp.zeros((patch, wanted.shape[1]), jnp.float32)
+            for k in range(ov):
+                hit = entries[:, k : k + 1] == wanted
+                total = total + jnp.where(hit, entries[:, ov + k : ov + k + 1], 0.0)
+            mixing[device] = (total * inverse).astype(bf)
+
+    def deposit(q):
+        weights = mixing[...].reshape(group * patch, -1)
+        cell_count = slab.shape[1]
+        for r in range(8):
+            rows = grads[:, pl.ds(q * 8 + r, 1)].reshape(group * patch, width)
+            made = lax.dot_general(
+                rows, weights, (((0,), (0,)), ((), ())), preferred_element_type=jnp.float32
+            ).astype(bf)
+            for t in range(tiles_here):
+                out[q * 8 + r, t * width : (t + 1) * width, :] = made[
+                    :, t * cell_count : (t + 1) * cell_count
+                ]
+
+    def step_body(k, carry):
+        @pl.when(k < chunks)
+        def _():
+            compute(k)
+            for send in own:
+                block_copy(k, *send).start()
+
+        @pl.when((k >= 1) & (k < chunks + 1))
+        def _():
+            forward(k - 1, relay)
+
+        @pl.when((k >= 2) & (k < chunks + 2))
+        def _():
+            forward(k - 2, last)
+
+        @pl.when(k == 2)
+        def _():
+            mix_tables()
+
+        @pl.when(k >= 3)
+        def _():
+            for source in final:
+                arrived(k - 3, source)
+            deposit(k - 3)
+
+        return carry
+
+    lax.fori_loop(0, chunks + 3, step_body, 0)
+
+    def drain(q, carry):
+        for send in own:
+            block_copy(q, *send).wait_send()
+        for source, sends in relay + last:
+            for send in sends:
+                block_copy(q, *send).wait_send()
+        return carry
+
+    lax.fori_loop(0, chunks, drain, 0)
+    for step in range(1, group):
+        table_copy(step).wait_send()
+
+
+def body_gather(
+    convergence, summary_cot, stem_w, down_w, block_w, plane_ids, tile_ids, lens_weight, slab_map
+):
+    sky_count, depth_count = lax.axis_size("sky"), lax.axis_size("depth")
+    group = sky_count * depth_count
+    patch, height, width = convergence.shape
+    tiles_here = TPD // depth_count
+    cells = slab_map.shape[0]
+    vmem = pl.BlockSpec(memory_space=pltpu.VMEM)
+    chunks = height // 8
+    return pl.pallas_call(
+        functools.partial(pencil_kernel, (sky_count, depth_count, sky_count * TPD)),
+        out_shape=jax.ShapeDtypeStruct((height, tiles_here * width, cells), jnp.bfloat16),
+        in_specs=[vmem] * 9,
+        out_specs=vmem,
+        scratch_shapes=[
+            pltpu.VMEM((group, height, patch, width), jnp.bfloat16),
+            pltpu.VMEM((group, patch, 128), jnp.float32),
+            pltpu.VMEM((8 * width, down_w.shape[0]), jnp.bfloat16),
+            pltpu.VMEM((group, patch, tiles_here * cells), jnp.bfloat16),
+            pltpu.SemaphoreType.DMA((group, chunks)),
+            pltpu.SemaphoreType.DMA((group, chunks)),
+            pltpu.SemaphoreType.DMA((group,)),
+            pltpu.SemaphoreType.DMA((group,)),
+        ],
+        compiler_params=pltpu.CompilerParams(
+            collective_id=0, has_side_effects=True, vmem_limit_bytes=50 * 2**20
+        ),
+        name="pencil",
+    )(
+        convergence,
+        summary_cot,
+        stem_w,
+        down_w,
+        block_w,
+        plane_ids,
+        tile_ids,
+        lens_weight,
+        slab_map.reshape(1, cells),
+    )
+
+
+def body(convergence, summary_cot, stem_w, down_w, block_w, plane_ids, *rest):
+    group = lax.axis_size("sky") * lax.axis_size("depth")
+    gathered = group * convergence.shape[0]
+    exchanged = 2 * plane_ids.size
+    form = body_gather if gathered <= exchanged else body_exchange
+    return form(convergence, summary_cot, stem_w, down_w, block_w, plane_ids, *rest)
+
+
 def solution(mesh):
     placed = (
         P(("group", "sky", "depth"), None, None),

time: 299 us -> 41.5 us (0.14)
  waiting for transfers between devices: 151 us -> 0 us
  local copies, waits for them, and re-layouts: 87.5 us -> 8.55 us
  Pallas kernels: 0 us -> 32.4 us
  matrix products: 30.2 us -> 0 us
  starting transfers between devices: 24.4 us -> 0 us
  other arithmetic: 3.42 us -> 0 us
    all_to_all x5 -> x0, waiting for transfers between devices: 151 us -> none  [the longest x1 90.9 us: body(): lax.all_to_all(outgoing, 'sky', split_axis=0, concat_axis=0, tiled=True)]
    pallas_call x0 -> x1, Pallas kernels: none -> 32.4 us  [body_gather(): pl.pallas_call(functools.partial(pencil_kernel, (sky_count, depth_count,...]
    dot_general x16 -> x0, matrix products: 30.2 us -> none  [the longest x7 13.9 us: summarize(): jnp.dot(block_w[layer, 0].T, stream.astype(jnp.bfloat16), preferred_eleme...]
    all_to_all x5 -> x0, starting transfers between devices: 24.4 us -> none  [the longest x1 5.42 us: body(): lax.all_to_all(out_slots, 'sky', split_axis=0, concat_axis=0, tiled=True)]
    convert_element_type x10 -> x0, local copies, waits for them, and re-layouts: 22.6 us -> none  [the longest x5 16.9 us: summarize(): jax.nn.silu(jnp.dot(stem_w.T, stem_in, preferred_element_type=jnp.float32))]
    all_to_all x6 -> x0, local copies, waits for them, and re-layouts: 15.9 us -> none  [the longest x1 6.09 us: body(): lax.all_to_all(plane_block.astype(jnp.bfloat16), 'depth', split_axis=2, c...]
    reshape x10 -> x0, local copies, waits for them, and re-layouts: 14.9 us -> none  [the longest x1 8.27 us: summarize(): coarse.transpose(0, 3, 5, 1, 2, 4)]
    transpose x2 -> x0, local copies, waits for them, and re-layouts: 7.92 us -> none  [the longest x1 7.22 us: summarize(): coarse.transpose(0, 3, 5, 1, 2, 4)]
  transfers between devices with their start and end apart: 5 -> 0, of which waited for: 3 -> 0; matrix products, arithmetic and copies ran while one was open for 25% -> 0% of each run, Pallas kernels for 0% -> 0%
where the time goes in v2:
time: 41.5 us; the launch traced here: 41 us
  Pallas kernels  32.4 us (78%)
  local copies, waits for them, and re-layouts  8.55 us (21%)
    pallas_call x1, Pallas kernels, body_gather(): pl.pallas_call(functools.partial(pencil_kernel, (sky_count, depth_count,...  32.4 us
    unnamed x19, local copies, waits for them, and re-layouts  8.55 us

profile of v2, /device:TPU:1, one launch (start us, length us, event | category | flops | bytes accessed | tf_op | source)
XLA Modules:
  0.0 41.0 jit_solution(9211232057119716072)
XLA Ops:
  0.0 0.0 copy-start
  0.0 1.2 %copy-done = bf16[4,2,256,256]{3,2,1,0:T(8,128)(2,1)S(1)} copy-done((bf16[4,2,256,256]{3,2,1,0:T(8,128)(2,1)S(1)}, bf16[4,2,256,256]{3,2,1,0:T(8,128)(2,1)}, u32[]{:S(2)}) %copy-start) | copy-done | bytes 1048600
  1.2 0.0 copy-start.1
  1.2 0.9 %copy-done.1 = f32[16,32,128]{2,1,0:T(8,128)S(1)} copy-done((f32[16,32,128]{2,1,0:T(8,128)S(1)}, f32[16,32,128]{2,1,0:T(8,128)}, u32[]{:S(2)}) %copy-start.1) | copy-done | bytes 262168
  2.2 0.0 copy-start.2
  2.2 0.9 %copy-done.2 = bf16[256,256]{1,0:T(8,128)(2,1)S(1)} copy-done((bf16[256,256]{1,0:T(8,128)(2,1)S(1)}, bf16[256,256]{1,0:T(8,128)(2,1)}, u32[]{:S(2)}) %copy-start.2) | copy-done | bytes 131096
  3.1 0.0 copy-start.3
  3.1 0.7 %copy-done.3 = f32[16,256]{1,0:T(8,128)S(1)} copy-done((f32[16,256]{1,0:T(8,128)S(1)}, f32[16,256]{1,0:T(8,128)}, u32[]{:S(2)}) %copy-start.3) | copy-done | bytes 16408
  3.8 0.0 copy-start.4
  3.8 0.7 %copy-done.4 = s32[16,16]{1,0:T(8,128)S(1)} copy-done((s32[16,16]{1,0:T(8,128)S(1)}, s32[16,16]{1,0:T(8,128)}, u32[]{:S(2)}) %copy-start.4) | copy-done | bytes 1048
  4.5 0.0 copy-start.5
  4.5 0.7 %copy-done.5 = s32[16,16]{1,0:T(8,128)S(1)} copy-done((s32[16,16]{1,0:T(8,128)S(1)}, s32[16,16]{1,0:T(8,128)}, u32[]{:S(2)}) %copy-start.5) | copy-done | bytes 1048
  5.2 0.0 copy-start.6
  5.2 0.7 %copy-done.6 = f32[16,16]{1,0:T(8,128)S(1)} copy-done((f32[16,16]{1,0:T(8,128)S(1)}, f32[16,16]{1,0:T(8,128)}, u32[]{:S(2)}) %copy-start.6) | copy-done | bytes 1048
  5.9 0.0 copy-start.7
  5.9 0.7 %copy-done.7 = bf16[16,64]{1,0:T(8,128)(2,1)S(1)} copy-done((bf16[16,64]{1,0:T(8,128)(2,1)S(1)}, bf16[16,64]{1,0:T(8,128)(2,1)}, u32[]{:S(2)}) %copy-start.7) | copy-done | bytes 2072
  6.6 0.0 copy-start.8
  6.6 0.7 %copy-done.8 = s32[128]{0:T(128)S(1)} copy-done((s32[128]{0:T(128)S(1)}, s32[128]{0:T(128)}, u32[]{:S(2)}) %copy-start.8) | copy-done | bytes 536
  7.2 32.4 %pencil.1 = bf16[32,256,128]{2,1,0:T(8,128)(2,1)S(1)} custom-call(f32[16,32,128]{2,1,0:T(8,128)S(1)} %copy-done.1, f32[16,256]{1,0:T(8,128)S(1)} %copy-done.3, bf16[16,64]{1,0:T(8,128)(2,1)S(1)} %copy-done.7, bf16[256,256]{1,0:T(8,128)(2,1)S(1)} %copy-done.2, bf16[4,2,256,256]{3,2,1,0:T(8,128)(2,1)S(1)} %copy-done, s32[16,16]{1,0:T(8,128)S(1)} %copy-done.4, ...), custom_call_target="tpu_custom_call" | custom-call | tf_op jit(solution)/shard_map/pencil/pallas_call | solution.py:399
  39.7 1.3 %copy.11 = bf16[32,256,128]{2,1,0:T(8,128)(2,1)} copy(bf16[32,256,128]{2,1,0:T(8,128)(2,1)S(1)} %pencil.1) | data formatting | bytes 4194304
Async XLA Ops:
  0.0 1.2 %copy-start = (bf16[4,2,256,256]{3,2,1,0:T(8,128)(2,1)S(1)}, bf16[4,2,256,256]{3,2,1,0:T(8,128)(2,1)}, u32[]{:S(2)}) copy-start(bf16[4,2,256,256]{3,2,1,0:T(8,128)(2,1)} %block_w.1) | copy-start | bytes 3145732
  1.2 0.9 %copy-start.1 = (f32[16,32,128]{2,1,0:T(8,128)S(1)}, f32[16,32,128]{2,1,0:T(8,128)}, u32[]{:S(2)}) copy-start(f32[16,32,128]{2,1,0:T(8,128)} %conv.1) | copy-start | bytes 786436
  2.2 0.9 %copy-start.2 = (bf16[256,256]{1,0:T(8,128)(2,1)S(1)}, bf16[256,256]{1,0:T(8,128)(2,1)}, u32[]{:S(2)}) copy-start(bf16[256,256]{1,0:T(8,128)(2,1)} %down_w.1) | copy-start | bytes 393220
  3.1 0.7 %copy-start.3 = (f32[16,256]{1,0:T(8,128)S(1)}, f32[16,256]{1,0:T(8,128)}, u32[]{:S(2)}) copy-start(f32[16,256]{1,0:T(8,128)} %cot.1) | copy-start | bytes 49156
  3.8 0.7 %copy-start.4 = (s32[16,16]{1,0:T(8,128)S(1)}, s32[16,16]{1,0:T(8,128)}, u32[]{:S(2)}) copy-start(s32[16,16]{1,0:T(8,128)} %planes.1) | copy-start | bytes 3076
  4.5 0.7 %copy-start.5 = (s32[16,16]{1,0:T(8,128)S(1)}, s32[16,16]{1,0:T(8,128)}, u32[]{:S(2)}) copy-start(s32[16,16]{1,0:T(8,128)} %tiles.1) | copy-start | bytes 3076
  5.2 0.7 %copy-start.6 = (f32[16,16]{1,0:T(8,128)S(1)}, f32[16,16]{1,0:T(8,128)}, u32[]{:S(2)}) copy-start(f32[16,16]{1,0:T(8,128)} %lens.1) | copy-start | bytes 3076
  5.9 0.7 %copy-start.7 = (bf16[16,64]{1,0:T(8,128)(2,1)S(1)}, bf16[16,64]{1,0:T(8,128)(2,1)}, u32[]{:S(2)}) copy-start(bf16[16,64]{1,0:T(8,128)(2,1)} %stem_w.1) | copy-start | bytes 6148
  6.6 0.7 %copy-start.8 = (s32[128]{0:T(128)S(1)}, s32[128]{0:T(128)}, u32[]{:S(2)}) copy-start(s32[128]{0:T(128)} %param.17) | copy-start | bytes 1540

commit v3 on v2

--- a/solution.py
+++ b/solution.py
@@ -130,6 +130,22 @@
 
 def pencil_kernel(
     sizes,
+    *refs,
+):
+    inputs, (out, *held), rest = refs[:9], refs[9:19], refs[19:]
+    load_sem, rest = rest[0], rest[1:]
+    loads = [
+        pltpu.make_async_copy(source, target, load_sem.at[i])
+        for i, (source, target) in enumerate(zip(inputs, held))
+    ]
+    for i in (5, 6, 7, 2, 0, 3, 4, 1, 8):
+        loads[i].start()
+    pencil_steps(sizes, loads, *held, out, *rest)
+
+
+def pencil_steps(
+    sizes,
+    loads,
     conv,
     cot,
     stem_w,
@@ -173,9 +189,12 @@
             barrier, inc=1, device_id={"sky": to_sky, "depth": to_depth}, device_id_type=MESH
         )
 
+    for i in (5, 6, 7):
+        loads[i].wait()
     table[me, :, 0:ov] = (planes[...] * tile_count + tiles[...]).astype(jnp.float32)
     table[me, :, ov : 2 * ov] = lens[...]
 
+    loads[2].wait()
     row = lax.broadcasted_iota(jnp.int32, (8 * width, patch), 0)
     tap = ((row >> (width.bit_length() - 1)) & 3) * 4 + (row & 3)
     pick = (tap == lax.broadcasted_iota(jnp.int32, (8 * width, patch), 1)).astype(bf)
@@ -206,7 +225,8 @@
     for step in range(1, group):
         table_copy(step).start()
 
-    positions = across * patch
+    for i in (0, 3, 4, 1, 8):
+        loads[i].wait()
     lane_group = lax.broadcasted_iota(jnp.int32, (patch, width), 1) >> 3
 
     def compute(q):
@@ -394,14 +414,26 @@
     patch, height, width = convergence.shape
     tiles_here = TPD // depth_count
     cells = slab_map.shape[0]
-    vmem = pl.BlockSpec(memory_space=pltpu.VMEM)
     chunks = height // 8
+    operands = (
+        convergence,
+        summary_cot,
+        stem_w,
+        down_w,
+        block_w,
+        plane_ids,
+        tile_ids,
+        lens_weight,
+        slab_map.reshape(1, cells),
+    )
     return pl.pallas_call(
         functools.partial(pencil_kernel, (sky_count, depth_count, sky_count * TPD)),
         out_shape=jax.ShapeDtypeStruct((height, tiles_here * width, cells), jnp.bfloat16),
-        in_specs=[vmem] * 9,
-        out_specs=vmem,
-        scratch_shapes=[
+        in_specs=[pl.BlockSpec(memory_space=pl.ANY)] * len(operands),
+        out_specs=pl.BlockSpec(memory_space=pltpu.VMEM),
+        scratch_shapes=[pltpu.VMEM(x.shape, x.dtype) for x in operands]
+        + [
+            pltpu.SemaphoreType.DMA((len(operands),)),
             pltpu.VMEM((group, height, patch, width), jnp.bfloat16),
             pltpu.VMEM((group, patch, 128), jnp.float32),
             pltpu.VMEM((8 * width, down_w.shape[0]), jnp.bfloat16),
@@ -412,20 +444,10 @@
             pltpu.SemaphoreType.DMA((group,)),
         ],
         compiler_params=pltpu.CompilerParams(
-            collective_id=0, has_side_effects=True, vmem_limit_bytes=50 * 2**20
+            collective_id=0, has_side_effects=True, vmem_limit_bytes=67043328
         ),
         name="pencil",
-    )(
-        convergence,
-        summary_cot,
-        stem_w,
-        down_w,
-        block_w,
-        plane_ids,
-        tile_ids,
-        lens_weight,
-        slab_map.reshape(1, cells),
-    )
+    )(*operands)
 
 
 def body(convergence, summary_cot, stem_w, down_w, block_w, plane_ids, *rest):

time: 41.5 us -> 37.3 us (0.90)
  local copies, waits for them, and re-layouts: 8.55 us -> 3.14 us
  Pallas kernels: 32.4 us -> 33.9 us
    unnamed x19 -> x1, local copies, waits for them, and re-layouts: 8.55 us -> 3.14 us
    pallas_call x1, Pallas kernels: 32.4 us -> 33.9 us  [body_gather(): pl.pallas_call(functools.partial(pencil_kernel, (sky_count, depth_count,...]
where the time goes in v3:
time: 37.3 us; the launch traced here: 37.1 us
  Pallas kernels  33.9 us (91%)
  local copies, waits for them, and re-layouts  3.14 us (8%)
    pallas_call x1, Pallas kernels, body_gather(): pl.pallas_call(functools.partial(pencil_kernel, (sky_count, depth_count,...  33.9 us
    unnamed x1, local copies, waits for them, and re-layouts  3.14 us

profile of v3, /device:TPU:1, one launch (start us, length us, event | category | flops | bytes accessed | tf_op | source)
XLA Modules:
  0.0 37.1 jit_solution(13899345225660080902)
XLA Ops:
  0.0 33.9 %pencil.1 = bf16[32,256,128]{2,1,0:T(8,128)(2,1)} custom-call(f32[16,32,128]{2,1,0:T(8,128)} %refs_0_.1, f32[16,256]{1,0:T(8,128)} %refs_1_.1, bf16[16,64]{1,0:T(8,128)(2,1)} %refs_2_.1, bf16[256,256]{1,0:T(8,128)(2,1)} %refs_3_.1, bf16[4,2,256,256]{3,2,1,0:T(8,128)(2,1)} %refs_4_.1, s32[16,16]{1,0:T(8,128)} %refs_5_.1, s32[16,16]{1,0:T(8,128)} %refs_6_.1, ...), custom_call_target="tpu_custom_call" | custom-call | tf_op jit(solution)/shard_map/pencil/pallas_call | solution.py:429
  33.9 3.1 %copy.11 = bf16[32,256,128]{2,1,0:T(8,128)(2,1)} copy(bf16[32,256,128]{2,1,0:T(8,128)(2,1)} %pencil.1) | data formatting | bytes 4194304

commit v4 on v3

--- a/solution.py
+++ b/solution.py
@@ -9,6 +9,7 @@
 
 PLANES = 64
 TPD = 8
+READY = 0
 
 
 def summarize(maps, stem_w, down_w, block_w):
@@ -157,13 +158,10 @@
     slab,
     out,
     grads,
-    table,
     taps,
     mixing,
     send_sem,
     recv_sem,
-    table_send,
-    table_recv,
 ):
     sky_count, depth_count, tile_count = sizes
     bf = jnp.bfloat16
@@ -191,8 +189,11 @@
 
     for i in (5, 6, 7):
         loads[i].wait()
-    table[me, :, 0:ov] = (planes[...] * tile_count + tiles[...]).astype(jnp.float32)
-    table[me, :, ov : 2 * ov] = lens[...]
+    rough = lens[...].astype(bf)
+    fine = (lens[...] - rough.astype(jnp.float32)).astype(bf)
+    ids = [planes[...].astype(jnp.float32).astype(bf), tiles[...].astype(jnp.float32).astype(bf)]
+    blank = jnp.zeros((patch, width - 4 * ov), bf)
+    grads[me, 0] = jnp.concatenate(ids + [rough, fine, blank], axis=1)
 
     loads[2].wait()
     row = lax.broadcasted_iota(jnp.int32, (8 * width, patch), 0)
@@ -208,22 +209,6 @@
     row_half = row >> (width.bit_length() + 1)
     same = (row_half == ((lane >> 1) & 1)) & (((row >> 2) & 1) == (lane & 1))
     taps[...] = jnp.where(same, spread, 0.0).astype(bf)
-
-    pl.semaphore_wait(barrier, group - 1)
-
-    def table_copy(step):
-        to_sky, to_depth = shifted(step // depth_count, step % depth_count)
-        return pltpu.make_async_remote_copy(
-            src_ref=table.at[me],
-            dst_ref=table.at[me],
-            send_sem=table_send.at[step],
-            recv_sem=table_recv.at[me],
-            device_id={"sky": to_sky, "depth": to_depth},
-            device_id_type=MESH,
-        )
-
-    for step in range(1, group):
-        table_copy(step).start()
 
     for i in (0, 3, 4, 1, 8):
         loads[i].wait()
@@ -260,10 +245,10 @@
             total = jnp.zeros((patch, width), jnp.float32)
             for b in range(across):
                 total = jnp.where(lane_group == b, back[b * patch : (b + 1) * patch], total)
-            grads[me, q * 8 + r] = total.astype(bf)
-
-    def block_copy(q, source, to_sky, to_depth, slot):
-        block = grads.at[source, pl.ds(q * 8, 8)]
+            grads[me, q * 8 + r + 1] = total.astype(bf)
+
+    def block_copy(first, q, source, to_sky, to_depth, slot):
+        block = grads.at[source, pl.ds(0, 9)] if first else grads.at[source, pl.ds(q * 8 + 1, 8)]
         return pltpu.make_async_remote_copy(
             src_ref=block,
             dst_ref=block,
@@ -312,26 +297,16 @@
 
     own, relay, last, final = plan()
 
-    def arrived(q, source):
-        block_copy(q, source, sky, partner, 0).wait_recv()
-
-    def forward(q, items):
+    def arrived(first, q, source):
+        block_copy(first, q, source, sky, partner, 0).wait_recv()
+
+    def forward(first, q, items):
         for source, sends in items:
-            arrived(q, source)
+            arrived(first, q, source)
             for send in sends:
-                block_copy(q, *send).start()
+                block_copy(first, q, *send).start()
 
     def mix_tables():
-        for step in range(1, group):
-            a, b = shifted(step // depth_count, step % depth_count)
-            pltpu.make_async_remote_copy(
-                src_ref=table.at[me],
-                dst_ref=table.at[index(a, b)],
-                send_sem=table_send.at[step],
-                recv_sem=table_recv.at[index(a, b)],
-                device_id={"sky": a, "depth": b},
-                device_id_type=MESH,
-            ).wait_recv()
         first_tile = (sky * TPD + depth * tiles_here).astype(jnp.float32)
         cells = slab[...].astype(jnp.float32)
         cell_count = cells.shape[1]
@@ -342,20 +317,22 @@
         )
         inverse = jnp.concatenate([1.0 / thickness] * tiles_here, axis=1)
 
-        @pl.loop(0, group)
+        @pl.loop(0, group, unroll=4)
         def _(device):
-            entries = table[device]
+            entries = grads[device, 0].astype(jnp.float32)
+            code = entries[:, 0:ov] * float(tile_count) + entries[:, ov : 2 * ov]
+            weight = entries[:, 2 * ov : 3 * ov] + entries[:, 3 * ov : 4 * ov]
             total = jnp.zeros((patch, wanted.shape[1]), jnp.float32)
             for k in range(ov):
-                hit = entries[:, k : k + 1] == wanted
-                total = total + jnp.where(hit, entries[:, ov + k : ov + k + 1], 0.0)
+                hit = code[:, k : k + 1] == wanted
+                total = total + jnp.where(hit, weight[:, k : k + 1], 0.0)
             mixing[device] = (total * inverse).astype(bf)
 
     def deposit(q):
         weights = mixing[...].reshape(group * patch, -1)
         cell_count = slab.shape[1]
         for r in range(8):
-            rows = grads[:, pl.ds(q * 8 + r, 1)].reshape(group * patch, width)
+            rows = grads[:, pl.ds(q * 8 + r + 1, 1)].reshape(group * patch, width)
             made = lax.dot_general(
                 rows, weights, (((0,), (0,)), ((), ())), preferred_element_type=jnp.float32
             ).astype(bf)
@@ -364,46 +341,45 @@
                     :, t * cell_count : (t + 1) * cell_count
                 ]
 
-    def step_body(k, carry):
-        @pl.when(k < chunks)
+    def send_own(first, q):
+        for send in own:
+            block_copy(first, q, *send).start()
+
+    def compute_step(k, carry):
+        compute(k)
+
+        @pl.when(k == READY)
         def _():
-            compute(k)
-            for send in own:
-                block_copy(k, *send).start()
-
-        @pl.when((k >= 1) & (k < chunks + 1))
+            pl.semaphore_wait(barrier, group - 1)
+            send_own(True, 0)
+            for q in range(1, READY + 1):
+                send_own(False, q)
+
+        @pl.when(k > READY)
         def _():
-            forward(k - 1, relay)
-
-        @pl.when((k >= 2) & (k < chunks + 2))
-        def _():
-            forward(k - 2, last)
-
-        @pl.when(k == 2)
-        def _():
+            send_own(False, k)
+
+        return carry
+
+    lax.fori_loop(0, chunks, compute_step, 0)
+    for q in range(chunks):
+        forward(q == 0, q, relay)
+        if q > 0:
+            forward(q == 1, q - 1, last)
+    for q in range(chunks):
+        if q == chunks - 2:
+            forward(False, chunks - 1, last)
+        for source in final:
+            arrived(q == 0, q, source)
+        if q == 0:
             mix_tables()
-
-        @pl.when(k >= 3)
-        def _():
-            for source in final:
-                arrived(k - 3, source)
-            deposit(k - 3)
-
-        return carry
-
-    lax.fori_loop(0, chunks + 3, step_body, 0)
-
-    def drain(q, carry):
+        deposit(q)
+    for q in range(chunks):
         for send in own:
-            block_copy(q, *send).wait_send()
+            block_copy(q == 0, q, *send).wait_send()
         for source, sends in relay + last:
             for send in sends:
-                block_copy(q, *send).wait_send()
-        return carry
-
-    lax.fori_loop(0, chunks, drain, 0)
-    for step in range(1, group):
-        table_copy(step).wait_send()
+                block_copy(q == 0, q, *send).wait_send()
 
 
 def body_gather(
@@ -434,14 +410,11 @@
         scratch_shapes=[pltpu.VMEM(x.shape, x.dtype) for x in operands]
         + [
             pltpu.SemaphoreType.DMA((len(operands),)),
-            pltpu.VMEM((group, height, patch, width), jnp.bfloat16),
-            pltpu.VMEM((group, patch, 128), jnp.float32),
+            pltpu.VMEM((group, height + 1, patch, width), jnp.bfloat16),
             pltpu.VMEM((8 * width, down_w.shape[0]), jnp.bfloat16),
             pltpu.VMEM((group, patch, tiles_here * cells), jnp.bfloat16),
             pltpu.SemaphoreType.DMA((group, chunks)),
             pltpu.SemaphoreType.DMA((group, chunks)),
-            pltpu.SemaphoreType.DMA((group,)),
-            pltpu.SemaphoreType.DMA((group,)),
         ],
         compiler_params=pltpu.CompilerParams(
             collective_id=0, has_side_effects=True, vmem_limit_bytes=67043328

time: 37.3 us -> 34.4 us (0.922)
  Pallas kernels: 33.9 us -> 31.1 us
    pallas_call x1, Pallas kernels: 33.9 us -> 31.1 us  [body_gather(): pl.pallas_call(functools.partial(pencil_kernel, (sky_count, depth_count,...]
where the time goes in v4:
time: 34.4 us; the launch traced here: 34.2 us
  Pallas kernels  31.1 us (90%)
  local copies, waits for them, and re-layouts  3.14 us (9%)
    pallas_call x1, Pallas kernels, body_gather(): pl.pallas_call(functools.partial(pencil_kernel, (sky_count, depth_count,...  31.1 us
    unnamed x1, local copies, waits for them, and re-layouts  3.14 us

profile of v4, /device:TPU:1, one launch (start us, length us, event | category | flops | bytes accessed | tf_op | source)
XLA Modules:
  0.0 34.2 jit_solution(11468134836500229404)
XLA Ops:
  0.0 31.1 %pencil.1 = bf16[32,256,128]{2,1,0:T(8,128)(2,1)} custom-call(f32[16,32,128]{2,1,0:T(8,128)} %refs_0_.1, f32[16,256]{1,0:T(8,128)} %refs_1_.1, bf16[16,64]{1,0:T(8,128)(2,1)} %refs_2_.1, bf16[256,256]{1,0:T(8,128)(2,1)} %refs_3_.1, bf16[4,2,256,256]{3,2,1,0:T(8,128)(2,1)} %refs_4_.1, s32[16,16]{1,0:T(8,128)} %refs_5_.1, s32[16,16]{1,0:T(8,128)} %refs_6_.1, ...), custom_call_target="tpu_custom_call" | custom-call | tf_op jit(solution)/shard_map/pencil/pallas_call | solution.py:405
  31.1 3.1 %copy.11 = bf16[32,256,128]{2,1,0:T(8,128)(2,1)} copy(bf16[32,256,128]{2,1,0:T(8,128)(2,1)} %pencil.1) | data formatting | bytes 4194304

commit v5 on v4

--- a/solution.py
+++ b/solution.py
@@ -10,6 +10,7 @@
 PLANES = 64
 TPD = 8
 READY = 0
+LAG = 2
 
 
 def summarize(maps, stem_w, down_w, block_w):
@@ -359,13 +360,22 @@
         def _():
             send_own(False, k)
 
+        for q in range(chunks - LAG):
+
+            @pl.when(k == q + LAG)
+            def _():
+                relay_step(q)
+
         return carry
 
-    lax.fori_loop(0, chunks, compute_step, 0)
-    for q in range(chunks):
+    def relay_step(q):
         forward(q == 0, q, relay)
         if q > 0:
             forward(q == 1, q - 1, last)
+
+    lax.fori_loop(0, chunks, compute_step, 0)
+    for q in range(chunks - LAG, chunks):
+        relay_step(q)
     for q in range(chunks):
         if q == chunks - 2:
             forward(False, chunks - 1, last)

time: 34.4 us -> 32.1 us (0.933)
  Pallas kernels: 31.1 us -> 28.8 us
    pallas_call x1, Pallas kernels: 31.1 us -> 28.8 us  [body_gather(): pl.pallas_call(functools.partial(pencil_kernel, (sky_count, depth_count,...]
where the time goes in v5:
time: 32.1 us; the launch traced here: 31.9 us
  Pallas kernels  28.8 us (90%)
  local copies, waits for them, and re-layouts  3.14 us (10%)
    pallas_call x1, Pallas kernels, body_gather(): pl.pallas_call(functools.partial(pencil_kernel, (sky_count, depth_count,...  28.8 us
    unnamed x1, local copies, waits for them, and re-layouts  3.14 us

profile of v5, /device:TPU:1, one launch (start us, length us, event | category | flops | bytes accessed | tf_op | source)
XLA Modules:
  0.0 31.9 jit_solution(4979054068615250911)
XLA Ops:
  0.0 28.8 %pencil.1 = bf16[32,256,128]{2,1,0:T(8,128)(2,1)} custom-call(f32[16,32,128]{2,1,0:T(8,128)} %refs_0_.1, f32[16,256]{1,0:T(8,128)} %refs_1_.1, bf16[16,64]{1,0:T(8,128)(2,1)} %refs_2_.1, bf16[256,256]{1,0:T(8,128)(2,1)} %refs_3_.1, bf16[4,2,256,256]{3,2,1,0:T(8,128)(2,1)} %refs_4_.1, s32[16,16]{1,0:T(8,128)} %refs_5_.1, s32[16,16]{1,0:T(8,128)} %refs_6_.1, ...), custom_call_target="tpu_custom_call" | custom-call | tf_op jit(solution)/shard_map/pencil/pallas_call | solution.py:415
  28.8 3.1 %copy.11 = bf16[32,256,128]{2,1,0:T(8,128)(2,1)} copy(bf16[32,256,128]{2,1,0:T(8,128)(2,1)} %pencil.1) | data formatting | bytes 4194304
